TPU v7x, 256 devices: a whole 4x4x8 slice. The times are simulated.
256 devices in a mesh: dp: 8 (over z), tensor: 32 (over x, y, core).
Axes of the slice: x: 4, y: 4, z: 8, core: 2. Of those that a mesh axis runs over, the one named last changes fastest.
Arguments:
- hidden: bfloat16 [16384, 2048], P(('dp', 'tensor')), may hold values from -190 to 190
- norm_gain: float32 [2048], replicated, may hold values from 0.1 to 1.9
- head_weight: bfloat16 [2048, 50304], P(None, 'tensor'), may hold values from -0.3 to 0.3
- value_weight: bfloat16 [2048], replicated, may hold values from -0.125 to 0.125
- token_ids: int32 [16384], P(('dp', 'tensor')), may hold values from 0 to 50303
- slot_mask: int32 [16384], P(('dp', 'tensor')), may hold values from 0 to 1, as said below
- lengths: int32 [8, 8], P('dp'), may hold values from 1 to 512, 2048 in all within a row
- request_order: int32 [64], P('dp'), may hold values from 0 to 63, each once
Outputs:
- token_logprob: float32 [16384], P(('dp', 'tensor'))
- token_entropy: float32 [16384], P(('dp', 'tensor'))
- token_value: float32 [16384], P(('dp', 'tensor'))
- request_score: float32 [64], P('dp')
Inputs may be any that keep to these rules, and one draw needn't show every extreme that they name: `slot_mask`: 0 or 1. Among the 64 slots of one device at most 48 are 1 and at least half of 48, rounded down; in every draw some device has exactly 48.
All inputs are finite; a program needn't handle non-finite values.
Results may differ from a plain program's by a relative error of at most 0.0029.
Values may be sent and summed in bfloat16 or wider, within the bound.
A program may use at most 64 MiB of HBM per device.

v0:
```python
import jax
import jax.numpy as jnp
from jax import lax
from jax.sharding import PartitionSpec as P

EPSILON = 1e-06


def merged_2(value, axis, join):
    pieces = jax.tree.map(lambda part: lax.all_gather(part, axis), value)
    head = jax.tree.map(lambda part: part[0], pieces)
    tail = jax.tree.map(lambda part: part[1:], pieces)
    subtotal, _ = lax.scan(lambda subtotal, share: (join(subtotal, share), None), head, tail)
    return subtotal


def combine_parts(lhs_part, rhs_part):
    row_peak = jnp.maximum(lhs_part[0], rhs_part[0])
    left_factor = jnp.exp(lhs_part[0] - row_peak)
    right_factor = jnp.exp(rhs_part[0] - row_peak)
    row_mass = left_factor * lhs_part[1] + right_factor * rhs_part[1]
    row_spread = left_factor * (
        lhs_part[2] + (lhs_part[0] - row_peak) * lhs_part[1]
    ) + right_factor * (rhs_part[2] + (rhs_part[0] - row_peak) * rhs_part[1])
    return (row_peak, row_mass, row_spread, lhs_part[3] + rhs_part[3])


def on_device(
    hidden, norm_gain, head_weight, value_weight, token_ids, slot_mask, lengths, request_order
):
    own_rows = hidden.shape[0]
    vocab_local = head_weight.shape[1]
    tensor_index = lax.axis_index("tensor")
    widened = hidden.astype(jnp.float32)
    inverse_rms = lax.rsqrt(jnp.mean(widened * widened, axis=1, keepdims=True) + EPSILON)
    normed = (widened * inverse_rms * norm_gain).astype(jnp.bfloat16)
    weight_mask = slot_mask.astype(jnp.float32)
    token_value = weight_mask * jnp.dot(normed, value_weight, preferred_element_type=jnp.float32)
    sent_count = normed.shape[0]
    columns = tensor_index * vocab_local + jnp.arange(vocab_local, dtype=jnp.int32)
    piece_rows = lax.all_gather(normed, "tensor", axis=0, tiled=True)
    piece_ids = lax.all_gather(token_ids, "tensor", axis=0, tiled=True)
    logits = jnp.dot(piece_rows, head_weight, preferred_element_type=jnp.float32)
    row_peak = jnp.max(logits, axis=1)
    shifted = logits - row_peak[:, None]
    weights = jnp.exp(shifted)
    row_mass = jnp.sum(weights, axis=1)
    row_spread = jnp.sum(weights * shifted, axis=1)
    row_target = jnp.sum(jnp.where(columns[None, :] == piece_ids[:, None], logits, 0.0), axis=1)
    updates = (row_peak, row_mass, row_spread, row_target)
    row_peak, row_mass, row_spread, row_target = tuple((update for update in updates))
    own_start = tensor_index * sent_count
    merged = merged_2((row_peak, row_mass, row_spread, row_target), "tensor", combine_parts)
    row_peak, row_mass, row_spread, row_target = [
        lax.dynamic_slice_in_dim(member, own_start, sent_count) for member in merged
    ]
    log_mass = jnp.log(row_mass)
    token_logprob = weight_mask * (row_target - row_peak - log_mass)
    token_entropy = weight_mask * (log_mass - row_spread / row_mass)
    request_count = lengths.shape[1]
    span_lengths = lengths[0]
    span_ends = jnp.cumsum(span_lengths)
    slot_ids = tensor_index * own_rows + jnp.arange(own_rows, dtype=jnp.int32)
    position = jnp.sum((slot_ids[:, None] >= span_ends[None, :]).astype(jnp.int32), axis=1)
    onehot = position[:, None] == jnp.arange(request_count, dtype=jnp.int32)[None, :]
    by_pos = jnp.sum(jnp.where(onehot, token_logprob[:, None], 0.0), axis=0) / span_lengths.astype(
        jnp.float32
    )
    all_requests = request_count * lax.axis_size("dp")
    route_table = request_order[:, None] == jnp.arange(all_requests, dtype=jnp.int32)[None, :]
    by_request = jnp.sum(jnp.where(route_table, by_pos[:, None], 0.0), axis=0)
    totals = lax.psum(by_request, ("dp", "tensor"))
    request_score = lax.dynamic_slice_in_dim(
        totals, lax.axis_index("dp") * request_count, request_count
    )
    return (token_logprob, token_entropy, token_value, request_score)


def solution(mesh):
    return jax.shard_map(
        on_device,
        mesh=mesh,
        in_specs=(
            P(("dp", "tensor"), None),
            P(),
            P(None, "tensor"),
            P(),
            P(("dp", "tensor")),
            P(("dp", "tensor")),
            P("dp", None),
            P("dp"),
        ),
        out_specs=(P(("dp", "tensor")), P(("dp", "tensor")), P(("dp", "tensor")), P("dp")),
        check_vma=False,
    )
```

profile of v0, /device:TPU:1, one launch (start us, length us, event | category | flops | bytes accessed | tf_op | source)
XLA Modules:
  0.0 278.3 jit_solution(18414183828398171453)
XLA Ops:
  7.2 0.0 all-gather.6.cloned.1.call-start
  7.2 1.1 fusion.2
  8.3 1.8 fusion.4
  10.1 0.0 all-gather.6.cloned.1.call-update
  10.2 0.8 reduce-window.8
  11.0 0.7 reshape.86
  11.7 1.3 dynamic-slice
  13.6 0.9 dynamic-update-slice
  14.5 14.7 %all-reduce = s32[2048]{0:T(1024)S(1)} all-reduce(s32[2048]{0:T(1024)S(1)} %dynamic-update-slice), channel_id=1, replica_groups=mesh['dp'=8,'tensor'=32] {'tensor'}, use_global_device_ids=true, to_apply=%add | all-reduce | flops 2048 | bytes 16384
  29.2 0.1 convert_reduce_fusion
  29.3 1.6 fusion.1
  30.9 41.9 %all-gather.6.cloned.1.call-done = bf16[2048,2048]{1,0:T(8,128)(2,1)} async-done(((bf16[64,2048]{1,0:T(8,128)(2,1)}), bf16[2048,2048]{1,0:T(8,128)(2,1)}) %all-gather.6.cloned.1.call-update) | async-done | bytes 8388624 | tf_op jit(solution)/shard_map/all_gather | solution.py:41
  72.9 18.4 %fusion.5 = (f32[2048]{0:T(1024)S(1)}, f32[2048,1572]{0,1:T(8,128)S(1)}) fusion(bf16[2048,2048]{1,0:T(8,128)(2,1)} %all-gather.6.cloned.1.call-done, bf16[2048,1572]{0,1:T(8,128)(2,1)} %param.12), kind=kOutput, calls=%fused_computation.28 | convolution fusion | flops 13190109184 | bytes 27713536 | tf_op jit(solution)/shard_map/dot_general | solution.py:43
  91.3 0.0 copy-start
  91.3 0.0 copy-start.2
  91.3 0.0 copy-start.3
  91.3 4.7 %fusion = (f32[2048]{0:T(1024)S(1)}, f32[2048]{0:T(1024)S(1)}, f32[2048]{0:T(1024)S(1)}) fusion(f32[2048,1572]{0,1:T(8,128)S(1)} %get-tuple-element.88, f32[2048]{0:T(1024)S(1)} %get-tuple-element.87, s32[2048]{0:T(1024)S(1)} %all-reduce, s32[1572]{0:T(1024)S(1)} %iota_add_fusion), kind=kLoop, calls=%fused_computation.8 | loop fusion | flops 22530048 | bytes 12925072 | tf_op jit(solution)/shard_map/reduce_sum | solution.py:48
  96.1 24.5 %all-gather.2 = f32[65536]{0:T(1024)S(1)} all-gather(f32[2048]{0:T(1024)S(1)} %get-tuple-element.58), channel_id=4, replica_groups=mesh['dp'=8,'tensor'=32] {'tensor'}, dimensions={0}, use_global_device_ids=true | all-gather | bytes 270336 | tf_op jit(solution)/shard_map/all_gather | solution.py:10
  120.6 22.6 %all-gather = f32[65536]{0:T(1024)S(1)} all-gather(f32[2048]{0:T(1024)S(1)} %get-tuple-element.87), channel_id=2, replica_groups=mesh['dp'=8,'tensor'=32] {'tensor'}, dimensions={0}, use_global_device_ids=true | all-gather | bytes 270336 | tf_op jit(solution)/shard_map/all_gather | solution.py:10
  143.2 24.1 %all-gather.1 = f32[65536]{0:T(1024)S(1)} all-gather(f32[2048]{0:T(1024)S(1)} %get-tuple-element.59), channel_id=3, replica_groups=mesh['dp'=8,'tensor'=32] {'tensor'}, dimensions={0}, use_global_device_ids=true | all-gather | bytes 270336 | tf_op jit(solution)/shard_map/all_gather | solution.py:10
  167.3 22.8 %all-gather.3 = f32[65536]{0:T(1024)S(1)} all-gather(f32[2048]{0:T(1024)S(1)} %get-tuple-element.60), channel_id=5, replica_groups=mesh['dp'=8,'tensor'=32] {'tensor'}, dimensions={0}, use_global_device_ids=true | all-gather | bytes 270336 | tf_op jit(solution)/shard_map/all_gather | solution.py:10
  190.3 4.3 %while.16 = (s32[]{:T(128)}, f32[2048]{0:T(1024)S(1)}, f32[2048]{0:T(1024)S(1)}, f32[2048]{0:T(1024)S(1)}, f32[2048]{0:T(1024)S(1)}, /*index=5*/f32[31,2048]{1,0...) while((s32[]{:T(128)}, f32[2048]{0:T(1024)S(1)}, ...), condition=%wide.region_6.7_spmd, body=%wide.region_5.6_spmd.sunk | while | flops 32770 | bytes 221301 | solution.py:13
  194.6 0.0 copy-done
  194.6 0.6 subtract_multiply_fusion
  195.2 0.0 copy-start.1
  195.2 0.1 select_reduce_fusion.2
  195.3 0.0 copy-done.2
  195.3 0.0 copy-done.3
  195.3 0.1 select_reduce_fusion.1
  195.4 75.4 %psum.7 = f32[64]{0:T(128)S(1)} all-reduce(f32[64]{0:T(128)S(1)} %select_reduce_fusion.1), channel_id=1, replica_groups=mesh['dp'=8,'tensor'=32] {'dp','tensor'}, use_global_device_ids=true, to_apply=%region_11.12 | all-reduce | flops 64 | bytes 512 | tf_op jit(solution)/shard_map/psum | solution.py:72
  270.9 0.6 dynamic_slice.32
  271.5 0.0 copy-done.1
  (203 shorter events, 2.7 us)
Async XLA Ops:
  7.2 65.7 %all-gather.6.cloned.1.call-start = ((), (), s32[]{:S(2)}) async-start(), calls=%async_computation | async-start | bytes 8650752 | tf_op jit(solution)/shard_map/all_gather | solution.py:41
  91.3 103.3 %copy-start = (s32[64]{0:T(128)S(1)}, s32[64]{0:T(128)}, u32[]{:S(2)}) copy-start(s32[64]{0:T(128)} %param.15) | copy-start | bytes 772
  91.3 104.0 %copy-start.2 = (s32[1,8]{1,0:T(1,128)S(1)}, s32[1,8]{1,0:T(1,128)}, u32[]{:S(2)}) copy-start(s32[1,8]{1,0:T(1,128)} %param.16) | copy-start | bytes 100
  91.3 104.0 %copy-start.3 = (s32[8]{0:T(128)S(1)}, s32[8]{0:T(128)}, u32[]{:S(2)}) copy-start(s32[8]{0:T(128)} %param.17) | copy-start | bytes 100
  195.2 76.3 %copy-start.1 = (f32[64]{0:T(128)}, f32[64]{0:T(128)S(1)}, u32[]{:S(2)}) copy-start(f32[64]{0:T(128)S(1)} %get-tuple-element.86) | copy-start | bytes 772
Sparse Core Ops, SparseCore 0:
  10.6 62.2 all-gather.5
where the time goes:
time: 279 us; the launch traced here: 278 us
  blocking collectives  184 us (66%)
  waiting for transfers between devices  42 us (15%)
  matrix products  20.1 us (7%)
  between operations  14.9 us (5%)
  other arithmetic  10.4 us (4%)
  local copies, waits for them, and re-layouts  5.11 us (2%)
    all_gather x4, blocking collectives, merged_2(): pieces = jax.tree.map(lambda part: lax.all_gather(part, axis), value)  93.9 us
    psum x1, blocking collectives, on_device(): totals = lax.psum(by_request, ('dp', 'tensor'))  75.4 us
    all_gather x1, waiting for transfers between devices, on_device(): piece_rows = lax.all_gather(normed, 'tensor', axis=0, tiled=True)  41.9 us
    dot_general x1, matrix products, on_device(): jnp.dot(piece_rows, head_weight, preferred_element_type=jnp.float32)  18.4 us
    unnamed x1, blocking collectives  14.7 us
  transfers between devices with their start and end apart: 1, of which 1 were waited for; matrix products, arithmetic and copies ran while one was open for 2% of the time, Pallas kernels for 0%

commit v1 on v0

--- a/solution.py
+++ b/solution.py
@@ -69,7 +69,8 @@
     all_requests = request_count * lax.axis_size("dp")
     route_table = request_order[:, None] == jnp.arange(all_requests, dtype=jnp.int32)[None, :]
     by_request = jnp.sum(jnp.where(route_table, by_pos[:, None], 0.0), axis=0)
-    totals = lax.psum(by_request, ("dp", "tensor"))
+    inner = lax.psum(by_request, "dp")
+    totals = lax.psum(inner, "tensor")
     request_score = lax.dynamic_slice_in_dim(
         totals, lax.axis_index("dp") * request_count, request_count
     )

time: 279 us -> 283 us (1.014)
  blocking collectives: 184 us -> 188 us
    psum x1 -> x2, blocking collectives: 75.4 us -> 79.6 us  [the longest x1 65.8 us: on_device(): totals = lax.psum(inner, 'tensor')]
where the time goes in v1:
time: 283 us; the launch traced here: 282 us
  blocking collectives  188 us (66%)
  waiting for transfers between devices  42 us (15%)
  matrix products  20.1 us (7%)
  between operations  14.9 us (5%)
  other arithmetic  10.4 us (4%)
  local copies, waits for them, and re-layouts  5.11 us (2%)
    all_gather x4, blocking collectives, merged_2(): pieces = jax.tree.map(lambda part: lax.all_gather(part, axis), value)  93.8 us
    psum x1, blocking collectives, on_device(): totals = lax.psum(inner, 'tensor')  65.8 us
    all_gather x1, waiting for transfers between devices, on_device(): piece_rows = lax.all_gather(normed, 'tensor', axis=0, tiled=True)  41.9 us
    dot_general x1, matrix products, on_device(): jnp.dot(piece_rows, head_weight, preferred_element_type=jnp.float32)  18.4 us
    unnamed x1, blocking collectives  14.7 us
    psum x1, blocking collectives, on_device(): inner = lax.psum(by_request, 'dp')  13.8 us
  transfers between devices with their start and end apart: 1, of which 1 were waited for; matrix products, arithmetic and copies ran while one was open for 2% of the time, Pallas kernels for 0%

profile of v1, /device:TPU:1, one launch (start us, length us, event | category | flops | bytes accessed | tf_op | source)
XLA Modules:
  0.0 282.3 jit_solution(14427987406260312339)
XLA Ops:
  7.2 0.0 all-gather.6.cloned.1.call-start
  7.2 1.1 fusion.2
  8.3 1.8 fusion.4
  10.1 0.0 all-gather.6.cloned.1.call-update
  10.2 0.8 reduce-window.8
  11.0 0.7 reshape.86
  11.7 1.3 dynamic-slice
  13.6 0.9 dynamic-update-slice
  14.5 14.7 %all-reduce = s32[2048]{0:T(1024)S(1)} all-reduce(s32[2048]{0:T(1024)S(1)} %dynamic-update-slice), channel_id=1, replica_groups=mesh['dp'=8,'tensor'=32] {'tensor'}, use_global_device_ids=true, to_apply=%add | all-reduce | flops 2048 | bytes 16384
  29.2 0.1 convert_reduce_fusion
  29.3 1.6 fusion.1
  30.9 41.9 %all-gather.6.cloned.1.call-done = bf16[2048,2048]{1,0:T(8,128)(2,1)} async-done(((bf16[64,2048]{1,0:T(8,128)(2,1)}), bf16[2048,2048]{1,0:T(8,128)(2,1)}) %all-gather.6.cloned.1.call-update) | async-done | bytes 8388624 | tf_op jit(solution)/shard_map/all_gather | solution.py:41
  72.9 18.4 %fusion.5 = (f32[2048]{0:T(1024)S(1)}, f32[2048,1572]{0,1:T(8,128)S(1)}) fusion(bf16[2048,2048]{1,0:T(8,128)(2,1)} %all-gather.6.cloned.1.call-done, bf16[2048,1572]{0,1:T(8,128)(2,1)} %param.12), kind=kOutput, calls=%fused_computation.28 | convolution fusion | flops 13190109184 | bytes 27713536 | tf_op jit(solution)/shard_map/dot_general | solution.py:43
  91.3 0.0 copy-start
  91.3 0.0 copy-start.2
  91.3 0.0 copy-start.3
  91.3 4.7 %fusion = (f32[2048]{0:T(1024)S(1)}, f32[2048]{0:T(1024)S(1)}, f32[2048]{0:T(1024)S(1)}) fusion(f32[2048,1572]{0,1:T(8,128)S(1)} %get-tuple-element.88, f32[2048]{0:T(1024)S(1)} %get-tuple-element.87, s32[2048]{0:T(1024)S(1)} %all-reduce, s32[1572]{0:T(1024)S(1)} %iota_add_fusion), kind=kLoop, calls=%fused_computation.8 | loop fusion | flops 22530048 | bytes 12925072 | tf_op jit(solution)/shard_map/reduce_sum | solution.py:48
  96.1 24.5 %all-gather.2 = f32[65536]{0:T(1024)S(1)} all-gather(f32[2048]{0:T(1024)S(1)} %get-tuple-element.58), channel_id=4, replica_groups=mesh['dp'=8,'tensor'=32] {'tensor'}, dimensions={0}, use_global_device_ids=true | all-gather | bytes 270336 | tf_op jit(solution)/shard_map/all_gather | solution.py:10
  120.6 22.6 %all-gather = f32[65536]{0:T(1024)S(1)} all-gather(f32[2048]{0:T(1024)S(1)} %get-tuple-element.87), channel_id=2, replica_groups=mesh['dp'=8,'tensor'=32] {'tensor'}, dimensions={0}, use_global_device_ids=true | all-gather | bytes 270336 | tf_op jit(solution)/shard_map/all_gather | solution.py:10
  143.2 24.1 %all-gather.1 = f32[65536]{0:T(1024)S(1)} all-gather(f32[2048]{0:T(1024)S(1)} %get-tuple-element.59), channel_id=3, replica_groups=mesh['dp'=8,'tensor'=32] {'tensor'}, dimensions={0}, use_global_device_ids=true | all-gather | bytes 270336 | tf_op jit(solution)/shard_map/all_gather | solution.py:10
  167.3 22.6 %all-gather.3 = f32[65536]{0:T(1024)S(1)} all-gather(f32[2048]{0:T(1024)S(1)} %get-tuple-element.60), channel_id=5, replica_groups=mesh['dp'=8,'tensor'=32] {'tensor'}, dimensions={0}, use_global_device_ids=true | all-gather | bytes 270336 | tf_op jit(solution)/shard_map/all_gather | solution.py:10
  190.1 4.3 %while.16 = (s32[]{:T(128)}, f32[2048]{0:T(1024)S(1)}, f32[2048]{0:T(1024)S(1)}, f32[2048]{0:T(1024)S(1)}, f32[2048]{0:T(1024)S(1)}, /*index=5*/f32[31,2048]{1,0...) while((s32[]{:T(128)}, f32[2048]{0:T(1024)S(1)}, ...), condition=%wide.region_6.7_spmd, body=%wide.region_5.6_spmd.sunk | while | flops 32770 | bytes 221301 | solution.py:13
  194.4 0.0 copy-done
  194.4 0.6 subtract_multiply_fusion
  195.0 0.1 select_reduce_fusion.2
  195.1 0.0 copy-done.2
  195.2 0.0 copy-done.3
  195.2 0.1 select_reduce_fusion.1
  195.3 13.8 %psum.14 = f32[64]{0:T(128)S(1)} all-reduce(f32[64]{0:T(128)S(1)} %select_reduce_fusion.1), channel_id=1, replica_groups=mesh['dp'=8,'tensor'=32] {'dp'}, use_global_device_ids=true, to_apply=%region_11.12 | all-reduce | flops 64 | bytes 512 | tf_op jit(solution)/shard_map/psum | solution.py:72
  209.0 65.8 %psum.15 = f32[64]{0:T(128)S(1)} all-reduce(f32[64]{0:T(128)S(1)} %psum.14), channel_id=1, replica_groups=mesh['dp'=8,'tensor'=32] {'tensor'}, use_global_device_ids=true, to_apply=%region_12.13 | all-reduce | flops 64 | bytes 512 | tf_op jit(solution)/shard_map/psum | solution.py:73
  274.9 0.6 dynamic_slice.32
  275.5 0.0 copy-done.1
  (204 shorter events, 2.7 us)
Async XLA Ops:
  7.2 65.7 %all-gather.6.cloned.1.call-start = ((), (), s32[]{:S(2)}) async-start(), calls=%async_computation | async-start | bytes 8650752 | tf_op jit(solution)/shard_map/all_gather | solution.py:41
  91.3 103.1 %copy-start = (s32[64]{0:T(128)S(1)}, s32[64]{0:T(128)}, u32[]{:S(2)}) copy-start(s32[64]{0:T(128)} %param.15) | copy-start | bytes 772
  91.3 103.8 %copy-start.2 = (s32[1,8]{1,0:T(1,128)S(1)}, s32[1,8]{1,0:T(1,128)}, u32[]{:S(2)}) copy-start(s32[1,8]{1,0:T(1,128)} %param.16) | copy-start | bytes 100
  91.3 103.8 %copy-start.3 = (s32[8]{0:T(128)S(1)}, s32[8]{0:T(128)}, u32[]{:S(2)}) copy-start(s32[8]{0:T(128)} %param.17) | copy-start | bytes 100
  195.0 80.4 %copy-start.1 = (f32[64]{0:T(128)}, f32[64]{0:T(128)S(1)}, u32[]{:S(2)}) copy-start(f32[64]{0:T(128)S(1)} %get-tuple-element.86) | copy-start | bytes 772
Sparse Core Ops, SparseCore 0:
  10.6 62.2 all-gather.5

commit v2 on v0

--- a/solution.py
+++ b/solution.py
@@ -69,7 +69,7 @@
     all_requests = request_count * lax.axis_size("dp")
     route_table = request_order[:, None] == jnp.arange(all_requests, dtype=jnp.int32)[None, :]
     by_request = jnp.sum(jnp.where(route_table, by_pos[:, None], 0.0), axis=0)
-    totals = lax.psum(by_request, ("dp", "tensor"))
+    totals = jnp.sum(lax.all_gather(by_request, ("dp", "tensor")), 0)
     request_score = lax.dynamic_slice_in_dim(
         totals, lax.axis_index("dp") * request_count, request_count
     )

time: 279 us -> 442 us (1.58)
  waiting for transfers between devices: 42 us -> 280 us
  blocking collectives: 184 us -> 109 us
    unnamed x1 -> x3, waiting for transfers between devices: 0.02 us -> 236 us
    psum x1 -> x0, blocking collectives: 75.4 us -> none  [on_device(): totals = lax.psum(by_request, ('dp', 'tensor'))]
  transfers between devices with their start and end apart: 1 -> 2, of which waited for: 1 -> 2; matrix products, arithmetic and copies ran while one was open for 2% -> 1% of each run, Pallas kernels for 0% -> 0%
where the time goes in v2:
time: 442 us
  waiting for transfers between devices  280 us (63%)
  blocking collectives  109 us (25%)
  matrix products  19.1 us (4%)
  between operations  14.9 us (3%)
  other arithmetic  10.4 us (2%)
  local copies, waits for them, and re-layouts  6.94 us (2%)
    unnamed x3, waiting for transfers between devices  236 us
    all_gather x4, blocking collectives, merged_2(): pieces = jax.tree.map(lambda part: lax.all_gather(part, axis), value)  93.9 us
    all_gather x1, waiting for transfers between devices, on_device(): piece_rows = lax.all_gather(normed, 'tensor', axis=0, tiled=True)  43.5 us
    dot_general x1, matrix products, on_device(): jnp.dot(piece_rows, head_weight, preferred_element_type=jnp.float32)  18.4 us
    unnamed x1, blocking collectives  14.7 us
  transfers between devices with their start and end apart: 2, of which 2 were waited for; matrix products, arithmetic and copies ran while one was open for 1% of the time, Pallas kernels for 0%

profile of v2, /device:TPU:1, one launch (start us, length us, event | category | flops | bytes accessed | tf_op | source)
XLA Modules:
  0.0 441.7 jit_solution(12960260263963013514)
XLA Ops:
  7.2 0.0 all-gather.7.cloned.1.call-start
  7.2 1.1 fusion.2
  8.3 1.8 fusion.4
  10.1 0.0 all-gather.7.cloned.1.call-update
  10.2 0.0 all-reduce.4.cloned.1.call-start
  10.2 1.3 dynamic-slice
  11.5 0.8 reduce-window.8
  12.3 0.7 reshape.89
  13.7 0.9 dynamic-update-slice
  14.5 14.7 %all-reduce = s32[2048]{0:T(1024)S(1)} all-reduce(s32[2048]{0:T(1024)S(1)} %dynamic-update-slice), channel_id=1, replica_groups=mesh['dp'=8,'tensor'=32] {'tensor'}, use_global_device_ids=true, to_apply=%add | all-reduce | flops 2048 | bytes 16384
  29.3 0.1 convert_reduce_fusion
  29.3 43.5 %all-gather.7.cloned.1.call-done = bf16[2048,2048]{1,0:T(8,128)(2,1)} async-done(((bf16[64,2048]{1,0:T(8,128)(2,1)}), bf16[2048,2048]{1,0:T(8,128)(2,1)}) %all-gather.7.cloned.1.call-update) | async-done | bytes 8388624 | tf_op jit(solution)/shard_map/all_gather | solution.py:41
  72.9 18.4 %fusion.5 = (f32[2048]{0:T(1024)S(1)}, f32[2048,1572]{0,1:T(8,128)S(1)}) fusion(bf16[2048,2048]{1,0:T(8,128)(2,1)} %all-gather.7.cloned.1.call-done, bf16[2048,1572]{0,1:T(8,128)(2,1)} %param.12), kind=kOutput, calls=%fused_computation.28 | convolution fusion | flops 13190109184 | bytes 27713536 | tf_op jit(solution)/shard_map/dot_general | solution.py:43
  91.3 0.0 copy-start.2
  91.3 0.0 copy-start.5
  91.3 4.7 %fusion = (f32[2048]{0:T(1024)S(1)}, f32[2048]{0:T(1024)S(1)}, f32[2048]{0:T(1024)S(1)}) fusion(f32[2048,1572]{0,1:T(8,128)S(1)} %get-tuple-element.88, f32[2048]{0:T(1024)S(1)} %get-tuple-element.87, s32[2048]{0:T(1024)S(1)} %all-reduce, s32[1572]{0:T(1024)S(1)} %iota_add_fusion), kind=kLoop, calls=%fused_computation.8 | loop fusion | flops 22530048 | bytes 12925072 | tf_op jit(solution)/shard_map/reduce_sum | solution.py:48
  96.1 24.5 %all-gather.2 = f32[65536]{0:T(1024)S(1)} all-gather(f32[2048]{0:T(1024)S(1)} %get-tuple-element.58), channel_id=4, replica_groups=mesh['dp'=8,'tensor'=32] {'tensor'}, dimensions={0}, use_global_device_ids=true | all-gather | bytes 270336 | tf_op jit(solution)/shard_map/all_gather | solution.py:10
  120.6 22.6 %all-gather = f32[65536]{0:T(1024)S(1)} all-gather(f32[2048]{0:T(1024)S(1)} %get-tuple-element.87), channel_id=2, replica_groups=mesh['dp'=8,'tensor'=32] {'tensor'}, dimensions={0}, use_global_device_ids=true | all-gather | bytes 270336 | tf_op jit(solution)/shard_map/all_gather | solution.py:10
  143.2 24.1 %all-gather.1 = f32[65536]{0:T(1024)S(1)} all-gather(f32[2048]{0:T(1024)S(1)} %get-tuple-element.59), channel_id=3, replica_groups=mesh['dp'=8,'tensor'=32] {'tensor'}, dimensions={0}, use_global_device_ids=true | all-gather | bytes 270336 | tf_op jit(solution)/shard_map/all_gather | solution.py:10
  167.4 22.8 %all-gather.3 = f32[65536]{0:T(1024)S(1)} all-gather(f32[2048]{0:T(1024)S(1)} %get-tuple-element.60), channel_id=5, replica_groups=mesh['dp'=8,'tensor'=32] {'tensor'}, dimensions={0}, use_global_device_ids=true | all-gather | bytes 270336 | tf_op jit(solution)/shard_map/all_gather | solution.py:10
  190.3 4.3 while.16
  194.6 0.6 subtract_multiply_fusion
  195.2 0.1 select_reduce_fusion.2
  195.4 0.1 select_reduce_fusion.1
  195.4 0.3 dynamic-update-slice.1
  195.7 0.6 copy-done.1
  196.3 0.0 all-reduce.4.cloned.1.call-update
  196.4 0.7 fusion.1
  197.1 236.2 %all-reduce.4.cloned.1.call-done = f32[16384]{0:T(1024)} async-done(((f32[16384]{0:T(1024)}), f32[16384]{0:T(1024)}) %all-reduce.4.cloned.1.call-update) | async-done | bytes 65552
  433.3 0.9 reshape.69
  434.2 0.1 reduce_sum.79
  434.3 0.6 dynamic_slice.32
  (213 shorter events, 2.7 us)
Async XLA Ops:
  7.2 65.7 %all-gather.7.cloned.1.call-start = ((), (), s32[]{:S(2)}) async-start(), calls=%async_computation | async-start | bytes 8650752 | tf_op jit(solution)/shard_map/all_gather | solution.py:41
  10.2 423.1 %all-reduce.4.cloned.1.call-start = ((), (), s32[]{:S(2)}) async-start(), calls=%async_computation.1 | async-start | bytes 131072
  91.3 103.3 %copy-start.2 = (s32[64]{0:T(128)S(1)}, s32[64]{0:T(128)}, u32[]{:S(2)}) copy-start(s32[64]{0:T(128)} %param.15) | copy-start | bytes 772
  91.3 104.0 %copy-start.4 = (s32[1,8]{1,0:T(1,128)S(1)}, s32[1,8]{1,0:T(1,128)}, u32[]{:S(2)}) copy-start(s32[1,8]{1,0:T(1,128)} %param.16) | copy-start | bytes 100
  91.3 104.0 %copy-start.5 = (s32[8]{0:T(128)S(1)}, s32[8]{0:T(128)}, u32[]{:S(2)}) copy-start(s32[8]{0:T(128)} %param.17) | copy-start | bytes 100
  91.3 105.0 %copy-start = (bf16[64,2048]{1,0:T(8,128)(2,1)S(1)}, bf16[64,2048]{1,0:T(8,128)(2,1)}, u32[]{:S(2)}) copy-start(bf16[64,2048]{1,0:T(8,128)(2,1)} %fusion.4) | copy-start | bytes 786436
  195.2 239.7 %copy-start.3 = (f32[64]{0:T(128)}, f32[64]{0:T(128)S(1)}, u32[]{:S(2)}) copy-start(f32[64]{0:T(128)S(1)} %get-tuple-element.86) | copy-start | bytes 772
  195.7 0.6 copy-start.1
Sparse Core Ops, SparseCore 0:
  10.6 62.2 all-gather.6
  196.5 236.7 all-reduce.3
